TPU v7x, 32 devices: a whole 2x2x4 slice. The times are simulated.
32 devices in a mesh: gx: 4 (over z), gy: 4 (over x, core), gz: 2 (over y).
Axes of the slice: x: 2, y: 2, z: 4, core: 2. Of those that a mesh axis runs over, the one named last changes fastest.
Arguments:
- activations: bfloat16 [1024, 8192], P('gy', 'gx'), may hold values from -0.5 to 0.5
- cotangent: bfloat16 [1024, 8192], P('gy', 'gx'), may hold values from -1.5 to 1.5
- gate_pre: bfloat16 [1024, 26624], P('gx', ('gy', 'gz')), may hold values from -6 to 6
- up_pre: bfloat16 [1024, 26624], P('gx', ('gy', 'gz')), may hold values from -6 to 6
- gate_weight: bfloat16 [8192, 26624], P('gx', ('gy', 'gz')), may hold values from -0.0625 to 0.0625
- up_weight: bfloat16 [8192, 26624], P('gx', ('gy', 'gz')), may hold values from -0.0625 to 0.0625
- down_weight: bfloat16 [26624, 8192], P(('gy', 'gz'), 'gx'), may hold values from -0.15625 to 0.15625
Outputs:
- input_grad: bfloat16 [1024, 8192], P('gy', 'gx')
- gate_grad: bfloat16 [8192, 26624], P('gx', ('gy', 'gz'))
- up_grad: bfloat16 [8192, 26624], P('gx', ('gy', 'gz'))
- down_grad: bfloat16 [26624, 8192], P(('gy', 'gz'), 'gx')
All inputs are finite; a program needn't handle non-finite values.
Results may differ from a plain program's by a relative error of at most 0.015.
Values may be sent and summed in bfloat16 or wider, within the bound.
A program may use at most 192 MiB of HBM per device.

v0:
```python
import jax
import jax.numpy as jnp
from jax import lax
from jax.sharding import PartitionSpec as P

over_rows = (((0,), (0,)), ((), ()))
over_cols = (((1,), (1,)), ((), ()))


def swiglu_grads(gate_in, up_in, grad_hidden):
    gate_val = gate_in.astype(jnp.float32)
    up_val = up_in.astype(jnp.float32)
    sigmoid = jax.nn.sigmoid(gate_val)
    hidden = (gate_val * sigmoid * up_val).astype(jnp.bfloat16)
    grad_gate = (grad_hidden * up_val * sigmoid * (1.0 + gate_val * (1.0 - sigmoid))).astype(
        jnp.bfloat16
    )
    grad_up = (grad_hidden * gate_val * sigmoid).astype(jnp.bfloat16)
    return (hidden, grad_gate, grad_up)


def input_terms(grad_gate, grad_up, gate_weight, up_weight):

    def compute(offset, amount):
        total = lax.dot_general(
            grad_gate, gate_weight, over_cols, preferred_element_type=jnp.float32
        )
        return total + lax.dot_general(
            grad_up, up_weight, over_cols, preferred_element_type=jnp.float32
        )

    return compute


def shards(activations, cotangent, gate_pre, up_pre, gate_weight, up_weight, down_weight):
    cotangent_all = lax.all_gather(cotangent, "gy", axis=0, tiled=True)
    gate_all, up_all = (
        lax.all_gather(gate_pre, "gx", axis=0, tiled=True),
        lax.all_gather(up_pre, "gx", axis=0, tiled=True),
    )
    local_sum = lax.dot_general(
        cotangent_all, down_weight, over_cols, preferred_element_type=jnp.float32
    )
    grad_hidden = lax.psum(local_sum, "gx")
    hidden, grad_gate, grad_up = swiglu_grads(gate_all, up_all, grad_hidden)
    down_grad = lax.dot_general(
        hidden, cotangent_all, over_rows, preferred_element_type=jnp.float32
    ).astype(jnp.bfloat16)
    segment = lax.all_gather(activations, "gy", axis=0, tiled=True)
    first = lax.dot_general(segment, grad_gate, over_rows, preferred_element_type=jnp.float32)
    second = lax.dot_general(segment, grad_up, over_rows, preferred_element_type=jnp.float32)
    row_count = activations.shape[0]
    terms = input_terms(grad_gate, grad_up, gate_weight, up_weight)
    share_rows = row_count // lax.axis_size("gz")
    input_share = lax.psum_scatter(
        terms(jnp.int32(0), lax.axis_size(("gy", "gz")) * share_rows),
        ("gy", "gz"),
        scatter_dimension=0,
        tiled=True,
    )
    input_grad = lax.all_gather(input_share.astype(jnp.bfloat16), "gz", axis=0, tiled=True)
    return (input_grad, first.astype(jnp.bfloat16), second.astype(jnp.bfloat16), down_grad)


def solution(mesh):
    in_specs = (
        P("gy", "gx"),
        P("gy", "gx"),
        P("gx", ("gy", "gz")),
        P("gx", ("gy", "gz")),
        P("gx", ("gy", "gz")),
        P("gx", ("gy", "gz")),
        P(("gy", "gz"), "gx"),
    )
    out_specs = (P("gy", "gx"), P("gx", ("gy", "gz")), P("gx", ("gy", "gz")), P(("gy", "gz"), "gx"))
    return jax.shard_map(shards, mesh=mesh, in_specs=in_specs, out_specs=out_specs, check_vma=False)
```

profile of v0, /device:TPU:0, one launch (start us, length us, event | category | flops | bytes accessed | tf_op | source)
XLA Modules:
  0.0 951.3 jit_solution(15693381875679629747)
XLA Ops:
  7.2 0.0 all-gather.6.cloned.1.call-start
  7.2 0.7 all-gather.6.cloned.1.call-update
  7.9 0.0 all-gather.10.cloned.1.call-start
  7.9 0.7 all-gather.10.cloned.1.call-update
  8.6 0.0 all-gather.8.cloned.1.call-start
  8.7 0.7 all-gather.8.cloned.1.call-update
  9.4 0.0 all-reduce.2.cloned.1.call-start
  9.4 37.3 %all-gather.6.cloned.1.call-done = bf16[1024,2048]{1,0:T(8,128)(2,1)} async-done(((bf16[256,2048]{1,0:T(8,128)(2,1)}), bf16[1024,2048]{1,0:T(8,128)(2,1)}) %all-gather.6.cloned.1.call-update) | async-done | bytes 4194320 | tf_op jit(solution)/shard_map/all_gather | solution.py:36
  46.8 22.5 %fusion.17 = f32[1024,3328]{1,0:T(8,128)} fusion(bf16[1024,2048]{1,0:T(8,128)(2,1)} %all-gather.6.cloned.1.call-done, bf16[3328,2048]{1,0:T(8,128)(2,1)} %param.13), kind=kOutput, calls=%fused_computation.24 | convolution fusion | flops 13958643712 | bytes 31457280 | tf_op jit(solution)/shard_map/dot_general | solution.py:41
  69.3 0.0 all-reduce.2.cloned.1.call-update
  69.3 0.0 all-gather.14.cloned.1.call-start
  69.4 0.5 all-gather.14.cloned.1.call-update
  69.9 0.2 reduce-scatter.2.cloned.1.call-start
  70.2 102.1 %all-gather.10.cloned.1.call-done = bf16[1024,3328]{1,0:T(8,128)(2,1)} async-done(((bf16[256,3328]{1,0:T(8,128)(2,1)}), bf16[1024,3328]{1,0:T(8,128)(2,1)}) %all-gather.10.cloned.1.call-update) | async-done | bytes 6815760 | tf_op jit(solution)/shard_map/all_gather | solution.py:38
  172.3 123.8 %all-gather.8.cloned.1.call-done = bf16[1024,3328]{1,0:T(8,128)(2,1)} async-done(((bf16[256,3328]{1,0:T(8,128)(2,1)}), bf16[1024,3328]{1,0:T(8,128)(2,1)}) %all-gather.8.cloned.1.call-update) | async-done | bytes 6815760 | tf_op jit(solution)/shard_map/all_gather | solution.py:39
  296.1 461.1 %all-reduce.2.cloned.1.call-done = f32[1024,3328]{1,0:T(8,128)} async-done(((f32[1024,3328]{1,0:T(8,128)}), f32[1024,3328]{1,0:T(8,128)}) %all-reduce.2.cloned.1.call-update) | async-done | bytes 13631504 | tf_op jit(solution)/shard_map/psum | solution.py:44
  757.1 12.2 %fusion.2 = bf16[1024,3328]{1,0:T(8,128)(2,1)S(1)} fusion(f32[1024,3328]{1,0:T(8,128)} %all-reduce.2.cloned.1.call-done, bf16[1024,3328]{1,0:T(8,128)(2,1)} %all-gather.8.cloned.1.call-done, bf16[1024,3328]{1,0:T(8,128)(2,1)} %all-gather.10.cloned.1.call-done), kind=kLoop, calls=%fused_computation.11 | loop fusion | flops 40894464 | bytes 34078720 | tf_op jit(solution)/shard_map/convert_element_type | solution.py:15
  769.3 0.0 copy-start
  769.3 2.9 copy-done
  772.2 18.1 %fusion.18 = f32[1024,2048]{1,0:T(8,128)} fusion(bf16[1024,3328]{1,0:T(8,128)(2,1)S(1)} %fusion.2, bf16[2048,3328]{1,0:T(8,128)(2,1)} %param.11), kind=kOutput, calls=%fused_computation.25 | convolution fusion | flops 13958643712 | bytes 28835840 | tf_op jit(solution)/shard_map/dot_general | solution.py:25
  790.3 24.1 %convolution_add_fusion = f32[1024,2048]{1,0:T(8,128)} fusion(f32[1024,2048]{1,0:T(8,128)} %fusion.18, bf16[2048,3328]{1,0:T(8,128)(2,1)} %param.12, f32[1024,3328]{1,0:T(8,128)} %all-reduce.2.cloned.1.call-done, bf16[1024,3328]{1,0:T(8,128)(2,1)} %all-gather.10.cloned.1.call-done), kind=kOutput, calls=%fused_computation.22 | convolution fusion | flops 13984595968 | bytes 50855936 | tf_op jit(solution)/shard_map/dot_general | solution.py:28
  814.4 0.0 reduce-scatter.2.cloned.1.call-update
  814.4 0.3 all-gather.12.cloned.1.call-start
  814.7 23.9 %convolution_convert_fusion = bf16[3328,2048]{1,0:T(8,128)(2,1)} fusion(bf16[1024,2048]{1,0:T(8,128)(2,1)} %all-gather.6.cloned.1.call-done, bf16[1024,3328]{1,0:T(8,128)(2,1)} %all-gather.8.cloned.1.call-done, bf16[1024,3328]{1,0:T(8,128)(2,1)} %all-gather.10.cloned.1.call-done), kind=kOutput, calls=%fused_computation.6 | convolution fusion | flops 13992722432 | bytes 31457280 | tf_op jit(solution)/shard_map/dot_general | solution.py:46
  838.6 23.5 %fusion.11 = bf16[2048,3328]{0,1:T(8,128)(2,1)} fusion(bf16[1024,2048]{1,0:T(8,128)(2,1)} %all-gather.14.cloned.1.call-done, f32[1024,3328]{1,0:T(8,128)} %all-reduce.2.cloned.1.call-done, bf16[1024,3328]{1,0:T(8,128)(2,1)} %all-gather.10.cloned.1.call-done), kind=kOutput, calls=%fused_computation.20 | convolution fusion | flops 13989314560 | bytes 38273024 | tf_op jit(solution)/shard_map/dot_general | solution.py:51
  862.1 22.0 %reduce-scatter.2.cloned.1.call-done = f32[128,2048]{1,0:T(8,128)} async-done(((f32[1024,2048]{1,0:T(8,128)}), f32[128,2048]{1,0:T(8,128)}) %reduce-scatter.2.cloned.1.call-update) | async-done | bytes 1048592 | tf_op jit(solution)/shard_map/reduce_scatter | solution.py:55
  884.1 2.1 convert_element_type.37
  886.2 0.0 all-gather.12.cloned.1.call-update
  886.2 21.0 %fusion.10 = bf16[2048,3328]{0,1:T(8,128)(2,1)} fusion(bf16[1024,3328]{1,0:T(8,128)(2,1)} %copy-done, bf16[1024,2048]{1,0:T(8,128)(2,1)} %all-gather.14.cloned.1.call-done), kind=kOutput, calls=%fused_computation.19 | convolution fusion | flops 13965459456 | bytes 24641536 | tf_op jit(solution)/shard_map/dot_general | solution.py:50
  907.3 17.4 %copy.11 = bf16[2048,3328]{1,0:T(8,128)(2,1)} copy(bf16[2048,3328]{0,1:T(8,128)(2,1)} %fusion.10) | data formatting | bytes 27262976
  924.7 17.4 %copy.12 = bf16[2048,3328]{1,0:T(8,128)(2,1)} copy(bf16[2048,3328]{0,1:T(8,128)(2,1)} %fusion.11) | data formatting | bytes 27262976
  942.2 2.3 copy.15
  (2 shorter events, 0.0 us)
Async XLA Ops:
  7.2 39.6 %all-gather.6.cloned.1.call-start = ((), (), s32[]{:S(2)}) async-start(), calls=%async_computation.1 | async-start | bytes 5242880 | tf_op jit(solution)/shard_map/all_gather | solution.py:36
  7.9 164.4 %all-gather.10.cloned.1.call-start = ((), (), s32[]{:S(2)}) async-start(), calls=%async_computation.4 | async-start | bytes 8519680 | tf_op jit(solution)/shard_map/all_gather | solution.py:38
  8.6 287.4 %all-gather.8.cloned.1.call-start = ((), (), s32[]{:S(2)}) async-start(), calls=%async_computation.3 | async-start | bytes 8519680 | tf_op jit(solution)/shard_map/all_gather | solution.py:39
  9.4 747.8 %all-reduce.2.cloned.1.call-start = ((), (), s32[]{:S(2)}) async-start(), calls=%async_computation.2 | async-start | bytes 27262976 | tf_op jit(solution)/shard_map/psum | solution.py:44
  69.3 769.3 %all-gather.14.cloned.1.call-start = ((), (), s32[]{:S(2)}) async-start(), calls=%async_computation.7 | async-start | bytes 5242880 | tf_op jit(solution)/shard_map/all_gather | solution.py:49
  69.9 814.2 %reduce-scatter.2.cloned.1.call-start = ((), (), s32[]{:S(2)}) async-start(), calls=%async_computation.5 | async-start | bytes 9437184 | tf_op jit(solution)/shard_map/reduce_scatter | solution.py:55
  769.3 2.9 copy-start
  814.4 127.7 %all-gather.12.cloned.1.call-start = ((), (), s32[]{:S(2)}) async-start(), calls=%async_computation.6 | async-start | bytes 1572864 | tf_op jit(solution)/shard_map/all_gather | solution.py:61
Sparse Core Ops, SparseCore 0:
  9.6 37.1 all-gather.5
  48.3 123.9 all-gather.9
  173.9 122.1 all-gather.7
  299.0 458.1 all-reduce.1
  758.6 33.3 all-gather.13
  814.6 69.5 reduce-scatter.1
  886.4 21.2 all-gather.11
where the time goes:
time: 952 us; the launch traced here: 951 us
  waiting for transfers between devices  749 us (79%)
  matrix products  133 us (14%)
  local copies, waits for them, and re-layouts  40.1 us (4%)
  other arithmetic  14.3 us (2%)
  between operations  14.1 us (1%)
    psum x1, waiting for transfers between devices, shards(): grad_hidden = lax.psum(local_sum, 'gx')  461 us
    all_gather x1, waiting for transfers between devices, shards(): lax.all_gather(up_pre, 'gx', axis=0, tiled=True)  124 us
    all_gather x1, waiting for transfers between devices, shards(): lax.all_gather(gate_pre, 'gx', axis=0, tiled=True)  102 us
    unnamed x5, local copies, waits for them, and re-layouts  40.1 us
    all_gather x1, waiting for transfers between devices, shards(): cotangent_all = lax.all_gather(cotangent, 'gy', axis=0, tiled=True)  37.3 us
    dot_general x1, matrix products, compute(): lax.dot_general(grad_up, up_weight, over_cols, preferred_element_type=jnp...  24.1 us
    dot_general x1, matrix products, shards(): lax.dot_general(hidden, cotangent_all, over_rows, preferred_element_type=...  23.9 us
    dot_general x1, matrix products, shards(): lax.dot_general(segment, grad_up, over_rows, preferred_element_type=jnp.f...  23.5 us
  transfers between devices with their start and end apart: 7, of which 5 were waited for; matrix products, arithmetic and copies ran while one was open for 19% of the time, Pallas kernels for 0%

commit v1 on v0

--- a/solution.py
+++ b/solution.py
@@ -41,7 +41,8 @@
     local_sum = lax.dot_general(
         cotangent_all, down_weight, over_cols, preferred_element_type=jnp.float32
     )
-    grad_hidden = lax.psum(local_sum, "gx")
+    pieces = lax.all_gather(local_sum, "gx", axis=0, tiled=False)
+    grad_hidden = pieces.sum(axis=0)
     hidden, grad_gate, grad_up = swiglu_grads(gate_all, up_all, grad_hidden)
     down_grad = lax.dot_general(
         hidden, cotangent_all, over_rows, preferred_element_type=jnp.float32

time: 952 us -> 1420 us (1.49)
  waiting for transfers between devices: 749 us -> 1190 us
  other arithmetic: 14.3 us -> 39.5 us
    all_gather x0 -> x1, waiting for transfers between devices: none -> 904 us  [shards(): pieces = lax.all_gather(local_sum, 'gx', axis=0, tiled=False)]
    psum x1 -> x0, waiting for transfers between devices: 461 us -> none  [shards(): grad_hidden = lax.psum(local_sum, 'gx')]
    reduce_sum x0 -> x1, other arithmetic: none -> 25.1 us  [shards(): grad_hidden = pieces.sum(axis=0)]
  transfers between devices with their start and end apart: 7 -> 7, of which waited for: 5 -> 5; matrix products, arithmetic and copies ran while one was open for 19% -> 13% of each run, Pallas kernels for 0% -> 0%
where the time goes in v1:
time: 1420 us
  waiting for transfers between devices  1190 us (84%)
  matrix products  133 us (9%)
  local copies, waits for them, and re-layouts  39.9 us (3%)
  other arithmetic  39.5 us (3%)
  between operations  14.4 us (1%)
    all_gather x1, waiting for transfers between devices, shards(): pieces = lax.all_gather(local_sum, 'gx', axis=0, tiled=False)  904 us
    all_gather x1, waiting for transfers between devices, shards(): lax.all_gather(up_pre, 'gx', axis=0, tiled=True)  124 us
    all_gather x1, waiting for transfers between devices, shards(): lax.all_gather(gate_pre, 'gx', axis=0, tiled=True)  99 us
    unnamed x5, local copies, waits for them, and re-layouts  39.9 us
    all_gather x1, waiting for transfers between devices, shards(): cotangent_all = lax.all_gather(cotangent, 'gy', axis=0, tiled=True)  38.8 us
  transfers between devices with their start and end apart: 7, of which 5 were waited for; matrix products, arithmetic and copies ran while one was open for 13% of the time, Pallas kernels for 0%

profile of v1, /device:TPU:0, one launch (start us, length us, event | category | flops | bytes accessed | tf_op | source)
XLA Modules:
  0.0 1417.4 jit_solution(8570504821461788977)
XLA Ops:
  7.2 0.0 all-gather.8.cloned.1.call-start
  7.2 0.7 all-gather.8.cloned.1.call-update
  7.9 0.0 all-gather.18.cloned.1.call-start
  7.9 38.8 %all-gather.8.cloned.1.call-done = bf16[1024,2048]{1,0:T(8,128)(2,1)} async-done(((bf16[256,2048]{1,0:T(8,128)(2,1)}), bf16[1024,2048]{1,0:T(8,128)(2,1)}) %all-gather.8.cloned.1.call-update) | async-done | bytes 4194320 | tf_op jit(solution)/shard_map/all_gather | solution.py:36
  46.8 22.5 %fusion.17 = f32[1024,3328]{1,0:T(8,128)} fusion(bf16[1024,2048]{1,0:T(8,128)(2,1)} %all-gather.8.cloned.1.call-done, bf16[3328,2048]{1,0:T(8,128)(2,1)} %param.13), kind=kOutput, calls=%fused_computation.24 | convolution fusion | flops 13958643712 | bytes 31457280 | tf_op jit(solution)/shard_map/dot_general | solution.py:41
  69.3 0.0 all-gather.18.cloned.1.call-update
  69.3 0.0 all-gather.12.cloned.1.call-start
  69.4 0.7 all-gather.12.cloned.1.call-update
  70.1 0.0 all-gather.10.cloned.1.call-start
  70.1 0.5 all-gather.10.cloned.1.call-update
  70.7 0.0 all-gather.16.cloned.1.call-start
  70.7 0.5 all-gather.16.cloned.1.call-update
  71.2 0.3 reduce-scatter.2.cloned.1.call-start
  71.6 904.0 %all-gather.18.cloned.1.call-done = f32[4096,3328]{1,0:T(8,128)} async-done(((f32[1024,3328]{1,0:T(8,128)}), f32[4096,3328]{1,0:T(8,128)}) %all-gather.18.cloned.1.call-update) | async-done | bytes 54525968 | tf_op jit(solution)/shard_map/all_gather | solution.py:44
  975.6 25.1 %reduce_sum.9 = f32[1024,3328]{1,0:T(8,128)} reduce(f32[4,1024,3328]{2,1,0:T(8,128)} %bitcast.14, f32[]{:T(128)} %constant.0.clone.1), dimensions={0}, to_apply=%region_0.0 | reduce | flops 10223616 | bytes 68157440 | tf_op jit(solution)/shard_map/reduce_sum | solution.py:45
  1000.7 99.0 %all-gather.12.cloned.1.call-done = bf16[1024,3328]{1,0:T(8,128)(2,1)} async-done(((bf16[256,3328]{1,0:T(8,128)(2,1)}), bf16[1024,3328]{1,0:T(8,128)(2,1)}) %all-gather.12.cloned.1.call-update) | async-done | bytes 6815760 | tf_op jit(solution)/shard_map/all_gather | solution.py:38
  1099.7 123.6 %all-gather.10.cloned.1.call-done = bf16[1024,3328]{1,0:T(8,128)(2,1)} async-done(((bf16[256,3328]{1,0:T(8,128)(2,1)}), bf16[1024,3328]{1,0:T(8,128)(2,1)}) %all-gather.10.cloned.1.call-update) | async-done | bytes 6815760 | tf_op jit(solution)/shard_map/all_gather | solution.py:39
  1223.3 12.3 fusion.2
  1235.6 2.7 copy-done
  1238.3 18.1 %fusion.18 = f32[1024,2048]{1,0:T(8,128)} fusion(bf16[1024,3328]{1,0:T(8,128)(2,1)S(1)} %fusion.2, bf16[2048,3328]{1,0:T(8,128)(2,1)} %param.11), kind=kOutput, calls=%fused_computation.25 | convolution fusion | flops 13958643712 | bytes 28835840 | tf_op jit(solution)/shard_map/dot_general | solution.py:25
  1256.5 24.0 %convolution_add_fusion = f32[1024,2048]{1,0:T(8,128)} fusion(f32[1024,2048]{1,0:T(8,128)} %fusion.18, bf16[2048,3328]{1,0:T(8,128)(2,1)} %param.12, f32[1024,3328]{1,0:T(8,128)} %reduce_sum.9, bf16[1024,3328]{1,0:T(8,128)(2,1)} %all-gather.12.cloned.1.call-done), kind=kOutput, calls=%fused_computation.22 | convolution fusion | flops 13984595968 | bytes 50855936 | tf_op jit(solution)/shard_map/dot_general | solution.py:28
  1280.5 0.0 reduce-scatter.2.cloned.1.call-update
  1280.5 0.6 all-gather.14.cloned.1.call-start
  1281.1 24.0 %convolution_convert_fusion = bf16[3328,2048]{1,0:T(8,128)(2,1)} fusion(bf16[1024,2048]{1,0:T(8,128)(2,1)} %all-gather.8.cloned.1.call-done, bf16[1024,3328]{1,0:T(8,128)(2,1)} %all-gather.10.cloned.1.call-done, bf16[1024,3328]{1,0:T(8,128)(2,1)} %all-gather.12.cloned.1.call-done), kind=kOutput, calls=%fused_computation.6 | convolution fusion | flops 13992722432 | bytes 31457280 | tf_op jit(solution)/shard_map/dot_general | solution.py:47
  1305.0 23.7 %fusion.11 = bf16[2048,3328]{0,1:T(8,128)(2,1)} fusion(bf16[1024,2048]{1,0:T(8,128)(2,1)} %all-gather.16.cloned.1.call-done, f32[1024,3328]{1,0:T(8,128)} %reduce_sum.9, bf16[1024,3328]{1,0:T(8,128)(2,1)} %all-gather.12.cloned.1.call-done), kind=kOutput, calls=%fused_computation.20 | convolution fusion | flops 13989314560 | bytes 38273024 | tf_op jit(solution)/shard_map/dot_general | solution.py:52
  1328.8 21.4 %reduce-scatter.2.cloned.1.call-done = f32[128,2048]{1,0:T(8,128)} async-done(((f32[1024,2048]{1,0:T(8,128)}), f32[128,2048]{1,0:T(8,128)}) %reduce-scatter.2.cloned.1.call-update) | async-done | bytes 1048592 | tf_op jit(solution)/shard_map/reduce_scatter | solution.py:56
  1350.1 2.1 convert_element_type.37
  1352.2 0.0 all-gather.14.cloned.1.call-update
  1352.2 20.9 %fusion.10 = bf16[2048,3328]{0,1:T(8,128)(2,1)} fusion(bf16[1024,3328]{1,0:T(8,128)(2,1)} %copy-done, bf16[1024,2048]{1,0:T(8,128)(2,1)} %all-gather.16.cloned.1.call-done), kind=kOutput, calls=%fused_computation.19 | convolution fusion | flops 13965459456 | bytes 24641536 | tf_op jit(solution)/shard_map/dot_general | solution.py:51
  1373.2 17.4 %copy.11 = bf16[2048,3328]{1,0:T(8,128)(2,1)} copy(bf16[2048,3328]{0,1:T(8,128)(2,1)} %fusion.10) | data formatting | bytes 27262976
  1390.6 17.4 %copy.12 = bf16[2048,3328]{1,0:T(8,128)(2,1)} copy(bf16[2048,3328]{0,1:T(8,128)(2,1)} %fusion.11) | data formatting | bytes 27262976
  1408.1 2.3 copy.14
  (3 shorter events, 0.0 us)
Async XLA Ops:
  7.2 39.6 %all-gather.8.cloned.1.call-start = ((), (), s32[]{:S(2)}) async-start(), calls=%async_computation.1 | async-start | bytes 5242880 | tf_op jit(solution)/shard_map/all_gather | solution.py:36
  7.9 967.7 %all-gather.18.cloned.1.call-start = ((), (), s32[]{:S(2)}) async-start(), calls=%async_computation.7 | async-start | bytes 68157440 | tf_op jit(solution)/shard_map/all_gather | solution.py:44
  69.3 1030.3 %all-gather.12.cloned.1.call-start = ((), (), s32[]{:S(2)}) async-start(), calls=%async_computation.3 | async-start | bytes 8519680 | tf_op jit(solution)/shard_map/all_gather | solution.py:38
  70.1 1153.2 %all-gather.10.cloned.1.call-start = ((), (), s32[]{:S(2)}) async-start(), calls=%async_computation.2 | async-start | bytes 8519680 | tf_op jit(solution)/shard_map/all_gather | solution.py:39
  70.7 1234.4 %all-gather.16.cloned.1.call-start = ((), (), s32[]{:S(2)}) async-start(), calls=%async_computation.6 | async-start | bytes 5242880 | tf_op jit(solution)/shard_map/all_gather | solution.py:50
  71.2 1278.9 %reduce-scatter.2.cloned.1.call-start = ((), (), s32[]{:S(2)}) async-start(), calls=%async_computation.4 | async-start | bytes 9437184 | tf_op jit(solution)/shard_map/reduce_scatter | solution.py:56
  1235.6 2.7 copy-start
  1280.5 127.5 %all-gather.14.cloned.1.call-start = ((), (), s32[]{:S(2)}) async-start(), calls=%async_computation.5 | async-start | bytes 1572864 | tf_op jit(solution)/shard_map/all_gather | solution.py:62
Sparse Core Ops, SparseCore 0:
  9.6 37.1 all-gather.7
  69.5 906.0 all-gather.17
  977.2 122.4 all-gather.11
  1101.1 122.1 all-gather.9
  1224.7 32.6 all-gather.15
  1280.6 69.4 reduce-scatter.1
  1352.4 21.2 all-gather.13
